TPU v7x, 32 devices: a whole 2x2x4 slice. The times are simulated.
32 devices in a mesh: groups: 2 (over y), blk: 8 (over z, x), heads: 2 (over core).
Axes of the slice: x: 2, y: 2, z: 4, core: 2. Of those that a mesh axis runs over, the one named last changes fastest.
Arguments:
- queries: bfloat16 [16, 64, 128], P(('groups', 'blk'), 'heads'), parts along dimension 0, may hold values from -256 to 256
- prefix_keys: bfloat16 [4096, 8, 128], P(('groups', 'blk'), 'heads'), parts along dimension 0, may hold values from -12 to 12
- prefix_values: bfloat16 [4096, 8, 128], P(('groups', 'blk'), 'heads'), parts along dimension 0, may hold values from -12 to 12
- suffix_pool: bfloat16 [48, 2, 16, 8, 128], P(('groups', 'blk'), None, None, 'heads'), parts along dimension 0, may hold values from -8.375 to 8.375
- page_owner: int32 [6, 8], P('groups'), parts along dimension 0, may hold values from 0 to 7, as said below
- page_slot: int32 [6, 8], P('groups'), parts along dimension 0, may hold values from 0 to 2, as said below
- suffix_len: int32 [6], P('groups'), parts along dimension 0, may hold values from 1 to 128, as said below
- row_request: int32 [16], P('groups'), parts along dimension 0, may hold values from 0 to 2, as said below
Outputs:
- attn_out: bfloat16 [16, 64, 128], P(('groups', 'blk'), 'heads'), parts along dimension 0
There are 2 independent parts, one for each index of `groups`. A program takes and returns all parts, laid end to end along the dimension named above; each array names one. Nothing has to cross between parts.
Inputs may be any that keep to these rules, and one draw needn't show every extreme that they name: `row_request`: rows 0 to 5 belong to one request, whose last 6 suffix tokens they are, in order; each later row is the only row of its request; every request has rows. `suffix_len`: counts the rows' own tokens; the prefill span's request has 6 or more, and some other request has exactly 128. Each request has one page on every blk index: page j lies on (page_owner[r, 0] + j) modulo the number of blk indices. `page_slot`: A local slot of the owner's pool; two requests never share a slot on one owner.
All inputs are finite; a program needn't handle non-finite values.
Results may differ from a plain program's by a relative error of at most 0.005.
Values may be sent and summed in bfloat16 or wider, within the bound.
A program may use at most 64 MiB of HBM per device.

v0:
```python
import math

import jax
import jax.numpy as jnp
from jax import lax
from jax.sharding import PartitionSpec as P


def merge_parts(first, second):
    first_max, first_sum, first_acc = first
    second_max, second_sum, second_acc = second
    highest = jnp.maximum(first_max, second_max)
    first_weight = jnp.exp(first_max - highest)
    second_weight = jnp.exp(second_max - highest)
    return (
        highest,
        first_sum * first_weight + second_sum * second_weight,
        first_acc * first_weight[..., None] + second_acc * second_weight[..., None],
    )


def prefix_part(query_rows, prefix_keys, prefix_values, kblock):
    row_count, qheads, head_dim = query_rows.shape
    kv_heads = prefix_keys.shape[1]
    group = qheads // kv_heads
    score_scale = 1.0 / math.sqrt(head_dim)
    grouped = query_rows.reshape(row_count, kv_heads, group, head_dim)
    block_total = prefix_keys.shape[0] // kblock
    key_blocks = prefix_keys.reshape(block_total, kblock, kv_heads, head_dim)
    value_blocks = prefix_values.reshape(block_total, kblock, kv_heads, head_dim)

    def key_step(running, blocks):
        run_max, run_sum, run_acc = running
        key_blk, value_blk = blocks
        scores = (
            jnp.einsum("rgqd,kgd->rgqk", grouped, key_blk, preferred_element_type=jnp.float32)
            * score_scale
        )
        new_max = jnp.maximum(run_max, jnp.max(scores, axis=-1))
        rescale = jnp.exp(run_max - new_max)
        probs = jnp.exp(scores - new_max[..., None])
        run_sum = run_sum * rescale + jnp.sum(probs, axis=-1)
        run_acc = run_acc * rescale[..., None] + jnp.einsum(
            "rgqk,kgd->rgqd",
            probs.astype(jnp.bfloat16),
            value_blk,
            preferred_element_type=jnp.float32,
        )
        return ((new_max, run_sum, run_acc), None)

    initial = (
        jnp.full((row_count, kv_heads, group), -1e30, jnp.float32),
        jnp.zeros((row_count, kv_heads, group), jnp.float32),
        jnp.zeros((row_count, kv_heads, group, head_dim), jnp.float32),
    )
    (run_max, run_sum, run_acc), _ = lax.scan(key_step, initial, (key_blocks, value_blocks))
    return (
        run_max.reshape(row_count, qheads),
        run_sum.reshape(row_count, qheads),
        run_acc.reshape(row_count, qheads, head_dim),
    )


def paged_part(query_rows, page_keys, page_values, visible):
    row_count, qheads, head_dim = query_rows.shape
    kv_heads = page_keys.shape[2]
    group = qheads // kv_heads
    score_scale = 1.0 / math.sqrt(head_dim)
    grouped = query_rows.reshape(row_count, kv_heads, group, head_dim)
    scores = (
        jnp.einsum("rgqd,rkgd->rgqk", grouped, page_keys, preferred_element_type=jnp.float32)
        * score_scale
    )
    shown = visible[:, None, None, :]
    scores = jnp.where(shown, scores, -1e30)
    highest = jnp.max(scores, axis=-1)
    probs = jnp.where(shown, jnp.exp(scores - highest[..., None]), 0.0)
    totals = jnp.sum(probs, axis=-1)
    mixed = jnp.einsum(
        "rgqk,rkgd->rgqd",
        probs.astype(jnp.bfloat16),
        page_values,
        preferred_element_type=jnp.float32,
    )
    return (
        highest.reshape(row_count, qheads),
        totals.reshape(row_count, qheads),
        mixed.reshape(row_count, qheads, head_dim),
    )


def on_device(
    queries, prefix_keys, prefix_values, suffix_pool, page_owner, page_slot, suffix_len, row_request
):
    block_count = lax.axis_size("blk")
    self_index = lax.axis_index("blk")
    rows_dev, qheads, head_dim = queries.shape
    page_len = suffix_pool.shape[2]
    row_count = row_request.shape[0]
    req_count = suffix_len.shape[0]
    kblock = min(prefix_keys.shape[0], 256)
    row_order = jnp.arange(row_count, dtype=jnp.int32)
    same_req = row_request[:, None] == row_request[None, :]
    later_rows = jnp.sum(
        (same_req & (row_order[None, :] > row_order[:, None])).astype(jnp.int32), axis=1
    )
    one_hot = (row_request[:, None] == jnp.arange(req_count, dtype=jnp.int32)[None, :]).astype(
        jnp.int32
    )
    limits = jnp.sum(one_hot * suffix_len[None, :], axis=1) - later_rows
    home_owner = jnp.sum(one_hot * page_owner[None, :, 0], axis=1)
    own_slot = jnp.sum(jnp.where(page_owner == self_index, page_slot, 0), axis=1)
    row_slot = jnp.sum(one_hot * own_slot[None, :], axis=1)
    page_index = (self_index - home_owner) % block_count
    all_rows = lax.all_gather(queries, "blk", axis=0, tiled=True)
    partial_value = prefix_part(all_rows, prefix_keys, prefix_values, kblock)
    first_token = page_index * page_len
    page_data = suffix_pool[row_slot]
    visible = (
        first_token[:, None] + jnp.arange(page_len, dtype=jnp.int32)[None, :] < limits[:, None]
    )
    partial_value = merge_parts(
        partial_value, paged_part(all_rows, page_data[:, 0], page_data[:, 1], visible)
    )
    sectioned = (
        partial_value[0].reshape(block_count, rows_dev, qheads),
        partial_value[1].reshape(block_count, rows_dev, qheads),
        partial_value[2].reshape(block_count, rows_dev, qheads, head_dim),
    )
    part_max = lax.all_to_all(sectioned[0], "blk", split_axis=0, concat_axis=0, tiled=True)
    part_sum = lax.all_to_all(sectioned[1], "blk", split_axis=0, concat_axis=0, tiled=True)
    part_acc = lax.all_to_all(sectioned[2], "blk", split_axis=0, concat_axis=0, tiled=True)
    highest = jnp.max(part_max, axis=0)
    weight = jnp.exp(part_max - highest[None])
    return (
        jnp.sum(part_acc * weight[..., None], axis=0)
        / jnp.sum(part_sum * weight, axis=0)[..., None]
    ).astype(jnp.bfloat16)


def solution(mesh):
    placed = (
        P(("groups", "blk"), "heads", None),
        P(("groups", "blk"), "heads", None),
        P(("groups", "blk"), "heads", None),
        P(("groups", "blk"), None, None, "heads", None),
        P("groups", None),
        P("groups", None),
        P("groups"),
        P("groups"),
    )
    return jax.shard_map(
        on_device,
        mesh=mesh,
        in_specs=placed,
        out_specs=P(("groups", "blk"), "heads", None),
        check_vma=False,
    )
```

profile of v0, /device:TPU:0, one launch (start us, length us, event | category | flops | bytes accessed | tf_op | source)
XLA Modules:
  0.0 72.5 jit_solution(9709522602568486579)
XLA Ops:
  0.0 0.7 copy-done.3
  0.7 0.1 slice_reduce_fusion
  0.8 0.5 copy-done.5
  1.4 0.2 convert_reduce_fusion
  1.6 0.1 select_reduce_fusion.1
  1.7 0.5 copy-done.6
  2.4 1.7 %gather_fusion = bf16[8,2,16,4,128]{4,3,2,1,0:T(4,128)(2,1)S(1)} fusion(bf16[3,2,16,4,128]{4,3,2,1,0:T(4,128)(2,1)} %param.11, s32[1024]{0:T(1024)S(1)} %pad_clamp_fusion), kind=kCustom, calls=%fused_computation | custom fusion | bytes 524320 | tf_op jit(solution)/shard_map/gather | solution.py:118
  4.1 0.6 copy-done.2
  4.7 32.3 %all_gather.3 = bf16[8,32,128]{2,1,0:T(8,128)(2,1)S(1)} all-gather(bf16[1,32,128]{2,1,0:T(8,128)(2,1)S(1)} %copy-done.2), channel_id=1, replica_groups=mesh['groups'=2,'blk'=8,'heads'=2] {'blk'}, dimensions={0}, use_global_device_ids=true | all-gather | bytes 73728 | tf_op jit(solution)/shard_map/all_gather | solution.py:115
  37.1 0.3 fusion.31
  37.5 0.2 fusion.13
  37.8 0.3 copy-done.1
  38.1 0.3 fusion.30
  38.4 0.2 fusion.9
  38.8 0.6 multiply_add_fusion
  39.4 5.5 %all-to-all-start.1 = ((f32[8,1,32]{2,1,0:T(1,128)}), f32[8,1,32]{2,1,0:T(1,128)S(1)}, u32[]{:S(2)}, u32[]{:S(2)}) async-start(f32[8,1,32]{2,1,0:T(1,128)} %bitcast.13), calls=%async_computation.1 | async-start | bytes 8192 | tf_op jit(solution)/shard_map/all_to_all | solution.py:130
  45.0 0.2 fusion.1
  45.3 6.1 %all-to-all-done.1 = f32[8,1,32]{2,1,0:T(1,128)S(1)} async-done(((f32[8,1,32]{2,1,0:T(1,128)}), f32[8,1,32]{2,1,0:T(1,128)S(1)}, u32[]{:S(2)}, u32[]{:S(2)}) %all-to-all-start.1) | async-done | bytes 1056 | tf_op jit(solution)/shard_map/all_to_all | solution.py:130
  51.4 3.3 %all-to-all-start.2 = ((f32[8,1,32]{2,1,0:T(1,128)}), f32[8,1,32]{2,1,0:T(1,128)S(1)}, u32[]{:S(2)}, u32[]{:S(2)}) async-start(f32[8,1,32]{2,1,0:T(1,128)} %bitcast.16), calls=%async_computation.2 | async-start | bytes 8192 | tf_op jit(solution)/shard_map/all_to_all | solution.py:131
  54.7 0.9 %fusion.6 = f32[8,1,32,128]{3,2,1,0:T(8,128)} fusion(bf16[8,1,16,4,128]{4,3,2,1,0:T(4,128)(2,1)S(1)} %get-tuple-element.34, f32[8,4,8,128]{3,2,0,1:T(8,128)S(1)} %fusion.1, f32[8,4,8,16]{3,2,1,0:T(8,128)S(1)} %get-tuple-element.42, f32[8,32]{1,0:T(8,128)S(1)} %get-tuple-element.38, f32[8,4,8]{2,1,0:T(4,128)S(1)} %get-tuple-element.41, ...), kind=kOutput, calls=%fused_computation.11 | convolution fusion | flops 1159168 | bytes 412800 | tf_op jit(solution)/shard_map/rgqk,rkgd->rgqd/dot_general | solution.py:79
  55.6 5.5 %all-to-all-done.2 = f32[8,1,32]{2,1,0:T(1,128)S(1)} async-done(((f32[8,1,32]{2,1,0:T(1,128)}), f32[8,1,32]{2,1,0:T(1,128)S(1)}, u32[]{:S(2)}, u32[]{:S(2)}) %all-to-all-start.2) | async-done | bytes 1056 | tf_op jit(solution)/shard_map/all_to_all | solution.py:131
  61.1 3.4 %all-to-all-start = ((f32[8,1,32,128]{3,2,1,0:T(8,128)}), f32[8,1,32,128]{3,2,1,0:T(8,128)S(1)}, u32[]{:S(2)}, u32[]{:S(2)}) async-start(f32[8,1,32,128]{3,2,1,0:T(8,128)} %fusion.6), calls=%async_computation | async-start | bytes 262144 | tf_op jit(solution)/shard_map/all_to_all | solution.py:132
  64.5 7.2 %all-to-all-done = f32[8,1,32,128]{3,2,1,0:T(8,128)S(1)} async-done(((f32[8,1,32,128]{3,2,1,0:T(8,128)}), f32[8,1,32,128]{3,2,1,0:T(8,128)S(1)}, u32[]{:S(2)}, u32[]{:S(2)}) %all-to-all-start) | async-done | bytes 131104 | tf_op jit(solution)/shard_map/all_to_all | solution.py:132
  71.8 0.7 fusion.20
  (29 shorter events, 1.0 us)
Async XLA Ops:
  0.0 45.0 %copy-start = (bf16[256,4,128]{2,1,0:T(4,128)(2,1)S(1)}, bf16[256,4,128]{2,1,0:T(4,128)(2,1)}, u32[]{:S(2)}) copy-start(bf16[256,4,128]{2,1,0:T(4,128)(2,1)} %param.10) | copy-start | bytes 786436
  0.0 0.7 %copy-start.3 = (s32[3,8]{1,0:T(4,128)S(1)}, s32[3,8]{1,0:T(4,128)}, u32[]{:S(2)}) copy-start(s32[3,8]{1,0:T(4,128)} %param.12) | copy-start | bytes 292
  0.7 0.7 copy-start.5
  0.7 0.8 %copy-start.4 = (s32[3,8]{1,0:T(4,128)S(1)}, s32[3,8]{1,0:T(4,128)}, u32[]{:S(2)}) copy-start(s32[3,8]{1,0:T(4,128)} %param.13) | copy-start | bytes 292
  1.6 0.7 copy-start.6
  4.0 0.7 copy-start.2
  37.1 1.0 %copy-start.1 = (bf16[256,4,128]{2,1,0:T(4,128)(2,1)S(1)}, bf16[256,4,128]{2,1,0:T(4,128)(2,1)}, u32[]{:S(2)}) copy-start(bf16[256,4,128]{2,1,0:T(4,128)(2,1)} %param.9) | copy-start | bytes 786436
  39.4 12.0 %all-to-all-start.1 = ((f32[8,1,32]{2,1,0:T(1,128)}), f32[8,1,32]{2,1,0:T(1,128)S(1)}, u32[]{:S(2)}, u32[]{:S(2)}) async-start(f32[8,1,32]{2,1,0:T(1,128)} %bitcast.13), calls=%async_computation.1 | async-start | bytes 8192 | tf_op jit(solution)/shard_map/all_to_all | solution.py:130
  51.4 9.7 %all-to-all-start.2 = ((f32[8,1,32]{2,1,0:T(1,128)}), f32[8,1,32]{2,1,0:T(1,128)S(1)}, u32[]{:S(2)}, u32[]{:S(2)}) async-start(f32[8,1,32]{2,1,0:T(1,128)} %bitcast.16), calls=%async_computation.2 | async-start | bytes 8192 | tf_op jit(solution)/shard_map/all_to_all | solution.py:131
  61.1 10.7 %all-to-all-start = ((f32[8,1,32,128]{3,2,1,0:T(8,128)}), f32[8,1,32,128]{3,2,1,0:T(8,128)S(1)}, u32[]{:S(2)}, u32[]{:S(2)}) async-start(f32[8,1,32,128]{3,2,1,0:T(8,128)} %fusion.6), calls=%async_computation | async-start | bytes 262144 | tf_op jit(solution)/shard_map/all_to_all | solution.py:132
where the time goes:
time: 73 us; the launch traced here: 72.5 us
  blocking collectives  32.3 us (44%)
  waiting for transfers between devices  18.8 us (26%)
  starting transfers between devices  12.1 us (17%)
  local copies, waits for them, and re-layouts  5.05 us (7%)
  other arithmetic  2.39 us (3%)
  matrix products  1.66 us (2%)
    all_gather x1, blocking collectives, on_device(): all_rows = lax.all_gather(queries, 'blk', axis=0, tiled=True)  32.3 us
    all_to_all x1, waiting for transfers between devices, on_device(): lax.all_to_all(sectioned[2], 'blk', split_axis=0, concat_axis=0, tiled=True)  7.22 us
    all_to_all x1, waiting for transfers between devices, on_device(): lax.all_to_all(sectioned[0], 'blk', split_axis=0, concat_axis=0, tiled=True)  6.07 us
    all_to_all x1, waiting for transfers between devices, on_device(): lax.all_to_all(sectioned[1], 'blk', split_axis=0, concat_axis=0, tiled=True)  5.5 us
    all_to_all x1, starting transfers between devices, on_device(): lax.all_to_all(sectioned[0], 'blk', split_axis=0, concat_axis=0, tiled=True)  5.46 us
    all_to_all x1, starting transfers between devices, on_device(): lax.all_to_all(sectioned[2], 'blk', split_axis=0, concat_axis=0, tiled=True)  3.37 us
    all_to_all x1, starting transfers between devices, on_device(): lax.all_to_all(sectioned[1], 'blk', split_axis=0, concat_axis=0, tiled=True)  3.31 us
    unnamed x14, local copies, waits for them, and re-layouts  2.68 us
  transfers between devices with their start and end apart: 3, of which 3 were waited for; matrix products, arithmetic and copies ran while one was open for 2% of the time, Pallas kernels for 0%

commit v1 on v0

v1 whole, which is shorter than its diff:
```python
import functools
import math

import jax
import jax.numpy as jnp
from jax import lax
from jax.experimental import pallas as pl
from jax.experimental.pallas import tpu as pltpu
from jax.sharding import PartitionSpec as P

MESH = pl.DeviceIdType.MESH
MASKED = -1e30
LANES = 128


def repeat(count, body, limit=16):
    if count <= limit:
        for step in range(count):
            body(step)
    else:

        def wrapped(step, carry):
            body(step)
            return carry

        lax.fori_loop(0, count, wrapped, 0)


def kernel(
    dims,
    q_ref,
    keys_ref,
    values_ref,
    pool_ref,
    owner_ref,
    slot_ref,
    len_ref,
    request_ref,
    out_ref,
    q_all,
    k_all,
    v_all,
    o_send,
    s_send,
    o_recv,
    s_recv,
    load_sem,
    q_send_sem,
    q_recv_sem,
    o_send_sem,
    o_recv_sem,
    s_send_sem,
    s_recv_sem,
):
    n, rows_dev, heads, head_dim, kv_heads, page_len, slots, chunk = dims
    rows = n * rows_dev
    group = heads // kv_heads
    page_rows = page_len * kv_heads
    prefix_rows = keys_ref.shape[0]
    total_rows = k_all.shape[0]
    suffix_rows = total_rows - prefix_rows
    exp_scale = math.log2(math.e) / math.sqrt(head_dim)
    me = lax.axis_index("blk")

    def peer(k):
        return lax.rem(me + k + 1, n)

    barrier = pltpu.get_barrier_semaphore()
    repeat(
        n - 1,
        lambda k: pl.semaphore_signal(
            barrier, inc=1, device_id={"blk": peer(k)}, device_id_type=MESH
        ),
    )

    own_rows = pl.ds(me * rows_dev, rows_dev)
    own_q = pltpu.make_async_copy(q_ref, q_all.at[own_rows], load_sem.at[0])
    own_q.start()
    prefix_k = pltpu.make_async_copy(keys_ref, k_all.at[pl.ds(0, prefix_rows)], load_sem.at[1])
    prefix_k.start()
    prefix_v = pltpu.make_async_copy(values_ref, v_all.at[pl.ds(0, prefix_rows)], load_sem.at[2])
    prefix_v.start()

    def page_copies(s):
        place = pl.ds(prefix_rows + s * page_rows, page_rows)
        return (
            pltpu.make_async_copy(
                pool_ref.at[pl.ds(2 * s * page_rows, page_rows)],
                k_all.at[place],
                load_sem.at[3 + 2 * s],
            ),
            pltpu.make_async_copy(
                pool_ref.at[pl.ds((2 * s + 1) * page_rows, page_rows)],
                v_all.at[place],
                load_sem.at[4 + 2 * s],
            ),
        )

    def start_page(s):
        for copy in page_copies(s):
            copy.start()

    def wait_page(s):
        for copy in page_copies(s):
            copy.wait()

    repeat(slots, start_page)
    used = prefix_rows + slots * page_rows
    if used < total_rows:
        pad = jnp.zeros((total_rows - used, head_dim), jnp.bfloat16)
        k_all[used:, :] = pad
        v_all[used:, :] = pad

    pl.semaphore_wait(barrier, n - 1)

    def query_copy(k, source):
        return pltpu.make_async_remote_copy(
            src_ref=q_ref,
            dst_ref=q_all.at[pl.ds(source * rows_dev, rows_dev)],
            send_sem=q_send_sem.at[k],
            recv_sem=q_recv_sem.at[source],
            device_id={"blk": peer(k)},
            device_id_type=MESH,
        )

    repeat(n - 1, lambda k: query_copy(k, me).start())

    def row_range(row):
        request = request_ref[row]
        later = jnp.int32(0)
        if rows <= 16:
            for other in range(rows):
                if isinstance(row, int) and other <= row:
                    continue
                later = later + jnp.where(
                    jnp.logical_and(request_ref[other] == request, other > row), 1, 0
                )
        else:
            later = lax.fori_loop(
                0,
                rows,
                lambda other, count: count
                + jnp.where(jnp.logical_and(request_ref[other] == request, other > row), 1, 0),
                later,
            )
        page = lax.rem(me - owner_ref[request, 0] + n, n)
        shown = len_ref[request] - later - page * page_len
        shown = jnp.minimum(jnp.maximum(shown, 0), page_len)
        low = slot_ref[request, page] * page_rows
        return low, low + shown * kv_heads

    head_of = lax.broadcasted_iota(jnp.int32, (heads, LANES), 0) // group
    lane = lax.broadcasted_iota(jnp.int32, (heads, LANES), 1)
    same = lax.rem(lane, kv_heads) == head_of
    head_ok = jnp.concatenate([same] * (total_rows // LANES), axis=1)
    suffix_ok = head_ok[:, prefix_rows:]
    column = lax.broadcasted_iota(jnp.int32, (heads, suffix_rows), 1)

    def row_mask(row):
        low, high = row_range(row)
        seen = jnp.logical_and(column >= low, column < high)
        return jnp.logical_and(seen, suffix_ok)

    prefix_k.wait()
    prefix_v.wait()
    repeat(slots, wait_page)
    own_q.wait()
    repeat(n - 1, lambda k: query_copy(k, peer(k)).wait_recv())

    def chunk_step(c):
        first = c * chunk
        q = q_all[pl.ds(first, chunk)].reshape(chunk * heads, head_dim)
        scores = lax.dot_general(
            q, k_all[...], (((1,), (1,)), ((), ())), preferred_element_type=jnp.float32
        )
        blocks = []
        for r in range(chunk):
            block = scores[r * heads : (r + 1) * heads]
            blocks.append(
                jnp.concatenate(
                    [
                        jnp.where(head_ok[:, :prefix_rows], block[:, :prefix_rows], MASKED),
                        jnp.where(row_mask(first + r), block[:, prefix_rows:], MASKED),
                    ],
                    axis=1,
                )
            )
        scores = jnp.concatenate(blocks, axis=0)
        highest = jnp.max(scores, axis=1, keepdims=True)
        probs = jnp.exp2((scores - highest) * exp_scale)
        total = jnp.sum(probs, axis=1, keepdims=True)
        mixed = jnp.dot(
            probs.astype(jnp.bfloat16), v_all[...], preferred_element_type=jnp.float32
        )
        o_send[pl.ds(first, chunk)] = (
            (mixed / total).astype(jnp.bfloat16).reshape(chunk, heads, head_dim)
        )
        wide = lax.broadcasted_iota(jnp.int32, (chunk * heads, LANES), 1)
        stats = jnp.where(wide == 0, highest, total).T
        for r in range(chunk):
            s_send[first + r, :, 0:heads] = stats[0:2, r * heads : (r + 1) * heads]

    repeat(rows // chunk, chunk_step, 1)

    def o_copy(k, target, source):
        return pltpu.make_async_remote_copy(
            src_ref=o_send.at[pl.ds(target * rows_dev, rows_dev)],
            dst_ref=o_recv.at[source],
            send_sem=o_send_sem.at[k],
            recv_sem=o_recv_sem.at[source],
            device_id={"blk": peer(k)},
            device_id_type=MESH,
        )

    def s_copy(k, target, source):
        return pltpu.make_async_remote_copy(
            src_ref=s_send.at[pl.ds(target * rows_dev, rows_dev)],
            dst_ref=s_recv.at[source],
            send_sem=s_send_sem.at[k],
            recv_sem=s_recv_sem.at[source],
            device_id={"blk": peer(k)},
            device_id_type=MESH,
        )

    def send(k):
        s_copy(k, peer(k), me).start()
        o_copy(k, peer(k), me).start()

    repeat(n - 1, send)
    o_recv[me] = o_send[own_rows]
    s_recv[me] = s_send[own_rows]

    def receive(k):
        s_copy(k, me, peer(k)).wait_recv()
        o_copy(k, me, peer(k)).wait_recv()

    repeat(n - 1, receive)

    for r in range(rows_dev):
        tops = s_recv[:, r, 0, :]
        sums = s_recv[:, r, 1, :]
        top = jnp.max(tops, axis=0, keepdims=True)
        weights = sums * jnp.exp2((tops - top) * exp_scale)
        weights = weights / jnp.sum(weights, axis=0, keepdims=True)
        columns = weights.T
        merged = jnp.zeros((heads, head_dim), jnp.float32)
        for p in range(n):
            merged = merged + o_recv[p, r].astype(jnp.float32) * columns[0:heads, p : p + 1]
        out_ref[r] = merged.astype(out_ref.dtype)

    def finish(k):
        query_copy(k, me).wait_send()
        s_copy(k, peer(k), me).wait_send()
        o_copy(k, peer(k), me).wait_send()

    repeat(n - 1, finish)


def on_device(
    queries, prefix_keys, prefix_values, suffix_pool, page_owner, page_slot, suffix_len, row_request
):
    n = lax.axis_size("blk")
    rows_dev, heads, head_dim = queries.shape
    kv_heads = prefix_keys.shape[1]
    slots, _, page_len = suffix_pool.shape[:3]
    rows = n * rows_dev
    chunk = math.gcd(rows, 8)
    prefix_rows = prefix_keys.shape[0] * kv_heads
    suffix_rows = -(-slots * page_len * kv_heads // LANES) * LANES
    total_rows = prefix_rows + suffix_rows
    dims = (n, rows_dev, heads, head_dim, kv_heads, page_len, slots, chunk)
    anywhere = pl.BlockSpec(memory_space=pl.ANY)
    scalar = pl.BlockSpec(memory_space=pltpu.SMEM)
    bf16, f32 = jnp.bfloat16, jnp.float32
    dma = pltpu.SemaphoreType.DMA
    return pl.pallas_call(
        functools.partial(kernel, dims),
        out_shape=jax.ShapeDtypeStruct(queries.shape, queries.dtype),
        in_specs=[anywhere] * 4 + [scalar] * 4,
        out_specs=pl.BlockSpec(memory_space=pltpu.VMEM),
        scratch_shapes=[
            pltpu.VMEM((rows, heads, head_dim), bf16),
            pltpu.VMEM((total_rows, head_dim), bf16),
            pltpu.VMEM((total_rows, head_dim), bf16),
            pltpu.VMEM((rows, heads, head_dim), bf16),
            pltpu.VMEM((rows, 2, LANES), f32),
            pltpu.VMEM((n, rows_dev, heads, head_dim), bf16),
            pltpu.VMEM((n, rows_dev, 2, LANES), f32),
            dma((3 + 2 * slots,)),
            dma((n - 1,)),
            dma((n,)),
            dma((n - 1,)),
            dma((n,)),
            dma((n - 1,)),
            dma((n,)),
        ],
        compiler_params=pltpu.CompilerParams(collective_id=0, has_side_effects=True),
    )(
        queries,
        prefix_keys.reshape(prefix_rows, head_dim),
        prefix_values.reshape(prefix_rows, head_dim),
        suffix_pool.reshape(slots * 2 * page_len * kv_heads, head_dim),
        page_owner,
        page_slot,
        suffix_len,
        row_request,
    )


def solution(mesh):
    placed = (
        P(("groups", "blk"), "heads", None),
        P(("groups", "blk"), "heads", None),
        P(("groups", "blk"), "heads", None),
        P(("groups", "blk"), None, None, "heads", None),
        P("groups", None),
        P("groups", None),
        P("groups"),
        P("groups"),
    )
    return jax.shard_map(
        on_device,
        mesh=mesh,
        in_specs=placed,
        out_specs=P(("groups", "blk"), "heads", None),
        check_vma=False,
    )
```

time: 73 us -> 19.2 us (0.26)
  blocking collectives: 32.3 us -> 0 us
  waiting for transfers between devices: 18.8 us -> 0 us
  Pallas kernels: 0 us -> 17.6 us
  starting transfers between devices: 12.1 us -> 0 us
  local copies, waits for them, and re-layouts: 5.05 us -> 1.3 us
  other arithmetic: 2.39 us -> 0 us
  matrix products: 1.66 us -> 0 us
    all_gather x1 -> x0, blocking collectives: 32.3 us -> none  [on_device(): all_rows = lax.all_gather(queries, 'blk', axis=0, tiled=True)]
    all_to_all x3 -> x0, waiting for transfers between devices: 18.8 us -> none  [the longest x1 7.22 us: on_device(): lax.all_to_all(sectioned[2], 'blk', split_axis=0, concat_axis=0, tiled=True)]
    pallas_call x0 -> x1, Pallas kernels: none -> 17.6 us  [on_device(): pl.pallas_call(functools.partial(kernel, dims), out_shape=jax.ShapeDtypeS...]
    all_to_all x3 -> x0, starting transfers between devices: 12.1 us -> none  [the longest x1 5.46 us: on_device(): lax.all_to_all(sectioned[0], 'blk', split_axis=0, concat_axis=0, tiled=True)]
    gather x1 -> x0, local copies, waits for them, and re-layouts: 1.66 us -> none  [on_device(): page_data = suffix_pool[row_slot]]
    dot_general x4 -> x0, matrix products: 1.66 us -> none  [the longest x1 0.88 us: paged_part(): jnp.einsum('rgqk,rkgd->rgqd', probs.astype(jnp.bfloat16), page_values, pr...]
    unnamed x14 -> x1, local copies, waits for them, and re-layouts: 2.68 us -> 1.3 us
    reduce_sum x7 -> x0, other arithmetic: 0.95 us -> none  [the longest x1 0.23 us: paged_part(): totals = jnp.sum(probs, axis=-1)]
  transfers between devices with their start and end apart: 3 -> 0, of which waited for: 3 -> 0; matrix products, arithmetic and copies ran while one was open for 2% -> 0% of each run, Pallas kernels for 0% -> 0%
where the time goes in v1:
time: 19.2 us; the launch traced here: 18.9 us
  Pallas kernels  17.6 us (92%)
  local copies, waits for them, and re-layouts  1.3 us (7%)
    pallas_call x1, Pallas kernels, on_device(): pl.pallas_call(functools.partial(kernel, dims), out_shape=jax.ShapeDtypeS...  17.6 us
    unnamed x1, local copies, waits for them, and re-layouts  1.3 us

profile of v1, /device:TPU:0, one launch (start us, length us, event | category | flops | bytes accessed | tf_op | source)
XLA Modules:
  0.0 18.9 jit_solution(3538991138127490658)
XLA Ops:
  0.0 17.6 %shard_map.82 = bf16[1,32,128]{2,1,0:T(8,128)(2,1)} custom-call(bf16[1,32,128]{2,1,0:T(8,128)(2,1)} %q_ref.1, bf16[1024,128]{1,0:T(8,128)(2,1)} %bitcast.3, bf16[1024,128]{1,0:T(8,128)(2,1)} %bitcast.4, bf16[384,128]{1,0:T(8,128)(2,1)} %bitcast.5, s32[3,8]{1,0:T(4,128)} %owner_ref.1, s32[3,8]{1,0:T(4,128)} %slot_ref.1, s32[3]{0:T(128)} %len_ref.1, s32[8]{0:T(128)} %request_ref.1), custom_call_target="tpu_custom_call" | custom-call | tf_op jit(solution)/shard_map/pallas_call | solution.py:276
  17.6 1.3 %copy.10 = bf16[1,32,128]{2,1,0:T(8,128)(2,1)} copy(bf16[1,32,128]{2,1,0:T(8,128)(2,1)} %shard_map.82) | data formatting | bytes 16384

commit v2 on v1

--- a/solution.py
+++ b/solution.py
@@ -32,11 +32,15 @@
     keys_ref,
     values_ref,
     pool_ref,
+    owner_hbm,
+    slot_hbm,
+    len_hbm,
+    request_hbm,
+    out_ref,
     owner_ref,
     slot_ref,
     len_ref,
     request_ref,
-    out_ref,
     q_all,
     k_all,
     v_all,
@@ -45,6 +49,7 @@
     o_recv,
     s_recv,
     load_sem,
+    table_sem,
     q_send_sem,
     q_recv_sem,
     o_send_sem,
@@ -73,6 +78,19 @@
         ),
     )
 
+    tables = [
+        pltpu.make_async_copy(source, place, table_sem.at[i])
+        for i, (source, place) in enumerate(
+            (
+                (owner_hbm, owner_ref),
+                (slot_hbm, slot_ref),
+                (len_hbm, len_ref),
+                (request_hbm, request_ref),
+            )
+        )
+    ]
+    for table in tables:
+        table.start()
     own_rows = pl.ds(me * rows_dev, rows_dev)
     own_q = pltpu.make_async_copy(q_ref, q_all.at[own_rows], load_sem.at[0])
     own_q.start()
@@ -161,6 +179,8 @@
         seen = jnp.logical_and(column >= low, column < high)
         return jnp.logical_and(seen, suffix_ok)
 
+    for table in tables:
+        table.wait()
     prefix_k.wait()
     prefix_v.wait()
     repeat(slots, wait_page)
@@ -192,9 +212,7 @@
         mixed = jnp.dot(
             probs.astype(jnp.bfloat16), v_all[...], preferred_element_type=jnp.float32
         )
-        o_send[pl.ds(first, chunk)] = (
-            (mixed / total).astype(jnp.bfloat16).reshape(chunk, heads, head_dim)
-        )
+        o_send[pl.ds(first, chunk)] = mixed.reshape(chunk, heads, head_dim)
         wide = lax.broadcasted_iota(jnp.int32, (chunk * heads, LANES), 1)
         stats = jnp.where(wide == 0, highest, total).T
         for r in range(chunk):
@@ -240,12 +258,12 @@
         tops = s_recv[:, r, 0, :]
         sums = s_recv[:, r, 1, :]
         top = jnp.max(tops, axis=0, keepdims=True)
-        weights = sums * jnp.exp2((tops - top) * exp_scale)
-        weights = weights / jnp.sum(weights, axis=0, keepdims=True)
+        weights = jnp.exp2((tops - top) * exp_scale)
+        weights = weights / jnp.sum(weights * sums, axis=0, keepdims=True)
         columns = weights.T
         merged = jnp.zeros((heads, head_dim), jnp.float32)
         for p in range(n):
-            merged = merged + o_recv[p, r].astype(jnp.float32) * columns[0:heads, p : p + 1]
+            merged = merged + o_recv[p, r] * columns[0:heads, p : p + 1]
         out_ref[r] = merged.astype(out_ref.dtype)
 
     def finish(k):
@@ -270,23 +288,27 @@
     total_rows = prefix_rows + suffix_rows
     dims = (n, rows_dev, heads, head_dim, kv_heads, page_len, slots, chunk)
     anywhere = pl.BlockSpec(memory_space=pl.ANY)
-    scalar = pl.BlockSpec(memory_space=pltpu.SMEM)
     bf16, f32 = jnp.bfloat16, jnp.float32
     dma = pltpu.SemaphoreType.DMA
     return pl.pallas_call(
         functools.partial(kernel, dims),
-        out_shape=jax.ShapeDtypeStruct(queries.shape, queries.dtype),
-        in_specs=[anywhere] * 4 + [scalar] * 4,
+        out_shape=pltpu.VMEM(queries.shape, queries.dtype),
+        in_specs=[anywhere] * 8,
         out_specs=pl.BlockSpec(memory_space=pltpu.VMEM),
         scratch_shapes=[
+            pltpu.SMEM(page_owner.shape, jnp.int32),
+            pltpu.SMEM(page_slot.shape, jnp.int32),
+            pltpu.SMEM(suffix_len.shape, jnp.int32),
+            pltpu.SMEM(row_request.shape, jnp.int32),
             pltpu.VMEM((rows, heads, head_dim), bf16),
             pltpu.VMEM((total_rows, head_dim), bf16),
             pltpu.VMEM((total_rows, head_dim), bf16),
-            pltpu.VMEM((rows, heads, head_dim), bf16),
+            pltpu.VMEM((rows, heads, head_dim), f32),
             pltpu.VMEM((rows, 2, LANES), f32),
-            pltpu.VMEM((n, rows_dev, heads, head_dim), bf16),
+            pltpu.VMEM((n, rows_dev, heads, head_dim), f32),
             pltpu.VMEM((n, rows_dev, 2, LANES), f32),
             dma((3 + 2 * slots,)),
+            dma((4,)),
             dma((n - 1,)),
             dma((n,)),
             dma((n - 1,)),

time: 19.2 us -> 17.2 us (0.90)
  Pallas kernels: 17.6 us -> 16.4 us
  local copies, waits for them, and re-layouts: 1.3 us -> 0.6 us
    pallas_call x1, Pallas kernels: 17.6 us -> 16.4 us  [on_device(): pl.pallas_call(functools.partial(kernel, dims), out_shape=pltpu.VMEM(quer...]
    unnamed x1, local copies, waits for them, and re-layouts: 1.3 us -> 0.6 us
where the time goes in v2:
time: 17.2 us; the launch traced here: 17 us
  Pallas kernels  16.4 us (95%)
  local copies, waits for them, and re-layouts  0.6 us (3%)
    pallas_call x1, Pallas kernels, on_device(): pl.pallas_call(functools.partial(kernel, dims), out_shape=pltpu.VMEM(quer...  16.4 us
    unnamed x1, local copies, waits for them, and re-layouts  0.6 us

profile of v2, /device:TPU:0, one launch (start us, length us, event | category | flops | bytes accessed | tf_op | source)
XLA Modules:
  0.0 17.0 jit_solution(13941271952311617448)
XLA Ops:
  0.0 16.4 %shard_map.82 = bf16[1,32,128]{2,1,0:T(8,128)(2,1)S(1)} custom-call(bf16[1,32,128]{2,1,0:T(8,128)(2,1)} %q_ref.1, bf16[1024,128]{1,0:T(8,128)(2,1)} %bitcast.3, bf16[1024,128]{1,0:T(8,128)(2,1)} %bitcast.4, bf16[384,128]{1,0:T(8,128)(2,1)} %bitcast.5, s32[3,8]{1,0:T(4,128)} %owner_hbm.1, s32[3,8]{1,0:T(4,128)} %slot_hbm.1, s32[3]{0:T(128)} %len_hbm.1, ...), custom_call_target="tpu_custom_call" | custom-call | tf_op jit(solution)/shard_map/pallas_call | solution.py:293
  16.4 0.6 %copy.10 = bf16[1,32,128]{2,1,0:T(8,128)(2,1)} copy(bf16[1,32,128]{2,1,0:T(8,128)(2,1)S(1)} %shard_map.82) | data formatting | bytes 16384

commit v3 on v2

--- a/solution.py
+++ b/solution.py
@@ -41,6 +41,8 @@
     slot_ref,
     len_ref,
     request_ref,
+    head_bias,
+    row_bias,
     q_all,
     k_all,
     v_all,
@@ -67,16 +69,29 @@
     exp_scale = math.log2(math.e) / math.sqrt(head_dim)
     me = lax.axis_index("blk")
 
-    def peer(k):
-        return lax.rem(me + k + 1, n)
+    half = n // 2
+    side = me // half
+    local = me - side * half
+
+    def far_peer(k):
+        return n - 1 - side * half - lax.rem(local + k, half)
+
+    def near_peer(k):
+        return side * half + lax.rem(local + k + 1, half)
+
+    def far_peers(body):
+        repeat(half, lambda k: body(k, far_peer(k)))
+
+    def near_peers(body):
+        repeat(half - 1, lambda k: body(half + k, near_peer(k)))
 
     barrier = pltpu.get_barrier_semaphore()
-    repeat(
-        n - 1,
-        lambda k: pl.semaphore_signal(
-            barrier, inc=1, device_id={"blk": peer(k)}, device_id_type=MESH
-        ),
-    )
+
+    def greet(k, peer):
+        pl.semaphore_signal(barrier, inc=1, device_id={"blk": peer}, device_id_type=MESH)
+
+    far_peers(greet)
+    near_peers(greet)
 
     tables = [
         pltpu.make_async_copy(source, place, table_sem.at[i])
@@ -123,25 +138,27 @@
             copy.wait()
 
     repeat(slots, start_page)
+    own_q.wait()
+    pl.semaphore_wait(barrier, n - 1)
+
+    def query_copy(k, peer, source):
+        return pltpu.make_async_remote_copy(
+            src_ref=q_all.at[own_rows],
+            dst_ref=q_all.at[pl.ds(source * rows_dev, rows_dev)],
+            send_sem=q_send_sem.at[k],
+            recv_sem=q_recv_sem.at[source],
+            device_id={"blk": peer},
+            device_id_type=MESH,
+        )
+
+    far_peers(lambda k, peer: query_copy(k, peer, me).start())
+    near_peers(lambda k, peer: query_copy(k, peer, me).start())
+
     used = prefix_rows + slots * page_rows
     if used < total_rows:
         pad = jnp.zeros((total_rows - used, head_dim), jnp.bfloat16)
         k_all[used:, :] = pad
         v_all[used:, :] = pad
-
-    pl.semaphore_wait(barrier, n - 1)
-
-    def query_copy(k, source):
-        return pltpu.make_async_remote_copy(
-            src_ref=q_ref,
-            dst_ref=q_all.at[pl.ds(source * rows_dev, rows_dev)],
-            send_sem=q_send_sem.at[k],
-            recv_sem=q_recv_sem.at[source],
-            device_id={"blk": peer(k)},
-            device_id_type=MESH,
-        )
-
-    repeat(n - 1, lambda k: query_copy(k, me).start())
 
     def row_range(row):
         request = request_ref[row]
@@ -169,40 +186,34 @@
 
     head_of = lax.broadcasted_iota(jnp.int32, (heads, LANES), 0) // group
     lane = lax.broadcasted_iota(jnp.int32, (heads, LANES), 1)
-    same = lax.rem(lane, kv_heads) == head_of
-    head_ok = jnp.concatenate([same] * (total_rows // LANES), axis=1)
-    suffix_ok = head_ok[:, prefix_rows:]
-    column = lax.broadcasted_iota(jnp.int32, (heads, suffix_rows), 1)
-
-    def row_mask(row):
+    head_tile = jnp.where(lax.rem(lane, kv_heads) == head_of, 0.0, MASKED)
+    for place in range(0, total_rows, LANES):
+        head_bias[:, place : place + LANES] = head_tile
+    column = lax.broadcasted_iota(jnp.int32, (1, suffix_rows), 1)
+    for table in tables:
+        table.wait()
+
+    def set_row_bias(row):
         low, high = row_range(row)
         seen = jnp.logical_and(column >= low, column < high)
-        return jnp.logical_and(seen, suffix_ok)
-
-    for table in tables:
-        table.wait()
+        row_bias[row] = jnp.where(seen, 0.0, MASKED)
+
+    repeat(rows, set_row_bias)
     prefix_k.wait()
     prefix_v.wait()
     repeat(slots, wait_page)
-    own_q.wait()
-    repeat(n - 1, lambda k: query_copy(k, peer(k)).wait_recv())
-
-    def chunk_step(c):
-        first = c * chunk
+
+    def chunk_step(first):
         q = q_all[pl.ds(first, chunk)].reshape(chunk * heads, head_dim)
         scores = lax.dot_general(
             q, k_all[...], (((1,), (1,)), ((), ())), preferred_element_type=jnp.float32
         )
         blocks = []
         for r in range(chunk):
-            block = scores[r * heads : (r + 1) * heads]
+            block = scores[r * heads : (r + 1) * heads] + head_bias[...]
             blocks.append(
                 jnp.concatenate(
-                    [
-                        jnp.where(head_ok[:, :prefix_rows], block[:, :prefix_rows], MASKED),
-                        jnp.where(row_mask(first + r), block[:, prefix_rows:], MASKED),
-                    ],
-                    axis=1,
+                    [block[:, :prefix_rows], block[:, prefix_rows:] + row_bias[first + r]], axis=1
                 )
             )
         scores = jnp.concatenate(blocks, axis=0)
@@ -218,41 +229,49 @@
         for r in range(chunk):
             s_send[first + r, :, 0:heads] = stats[0:2, r * heads : (r + 1) * heads]
 
-    repeat(rows // chunk, chunk_step, 1)
-
-    def o_copy(k, target, source):
+    def o_copy(k, peer, target, source):
         return pltpu.make_async_remote_copy(
             src_ref=o_send.at[pl.ds(target * rows_dev, rows_dev)],
             dst_ref=o_recv.at[source],
             send_sem=o_send_sem.at[k],
             recv_sem=o_recv_sem.at[source],
-            device_id={"blk": peer(k)},
+            device_id={"blk": peer},
             device_id_type=MESH,
         )
 
-    def s_copy(k, target, source):
+    def s_copy(k, peer, target, source):
         return pltpu.make_async_remote_copy(
             src_ref=s_send.at[pl.ds(target * rows_dev, rows_dev)],
             dst_ref=s_recv.at[source],
             send_sem=s_send_sem.at[k],
             recv_sem=s_recv_sem.at[source],
-            device_id={"blk": peer(k)},
+            device_id={"blk": peer},
             device_id_type=MESH,
         )
 
-    def send(k):
-        s_copy(k, peer(k), me).start()
-        o_copy(k, peer(k), me).start()
-
-    repeat(n - 1, send)
+    def send(k, peer):
+        s_copy(k, peer, peer, me).start()
+        o_copy(k, peer, peer, me).start()
+
+    def attend(which):
+        first = which * half * rows_dev
+        repeat(half * rows_dev // chunk, lambda c: chunk_step(first + c * chunk), 1)
+
+    near_peers(lambda k, peer: query_copy(k, peer, peer).wait_recv())
+    attend(side)
+    near_peers(send)
     o_recv[me] = o_send[own_rows]
     s_recv[me] = s_send[own_rows]
-
-    def receive(k):
-        s_copy(k, me, peer(k)).wait_recv()
-        o_copy(k, me, peer(k)).wait_recv()
-
-    repeat(n - 1, receive)
+    far_peers(lambda k, peer: query_copy(k, peer, peer).wait_recv())
+    attend(1 - side)
+    far_peers(send)
+
+    def receive(k, peer):
+        s_copy(k, peer, me, peer).wait_recv()
+        o_copy(k, peer, me, peer).wait_recv()
+
+    near_peers(receive)
+    far_peers(receive)
 
     for r in range(rows_dev):
         tops = s_recv[:, r, 0, :]
@@ -266,12 +285,13 @@
             merged = merged + o_recv[p, r] * columns[0:heads, p : p + 1]
         out_ref[r] = merged.astype(out_ref.dtype)
 
-    def finish(k):
-        query_copy(k, me).wait_send()
-        s_copy(k, peer(k), me).wait_send()
-        o_copy(k, peer(k), me).wait_send()
-
-    repeat(n - 1, finish)
+    def finish(k, peer):
+        query_copy(k, peer, me).wait_send()
+        s_copy(k, peer, peer, me).wait_send()
+        o_copy(k, peer, peer, me).wait_send()
+
+    far_peers(finish)
+    near_peers(finish)
 
 
 def on_device(
@@ -282,7 +302,7 @@
     kv_heads = prefix_keys.shape[1]
     slots, _, page_len = suffix_pool.shape[:3]
     rows = n * rows_dev
-    chunk = math.gcd(rows, 8)
+    chunk = math.gcd(rows // 2, 4)
     prefix_rows = prefix_keys.shape[0] * kv_heads
     suffix_rows = -(-slots * page_len * kv_heads // LANES) * LANES
     total_rows = prefix_rows + suffix_rows
@@ -300,6 +320,8 @@
             pltpu.SMEM(page_slot.shape, jnp.int32),
             pltpu.SMEM(suffix_len.shape, jnp.int32),
             pltpu.SMEM(row_request.shape, jnp.int32),
+            pltpu.VMEM((heads, total_rows), f32),
+            pltpu.VMEM((rows, 1, suffix_rows), f32),
             pltpu.VMEM((rows, heads, head_dim), bf16),
             pltpu.VMEM((total_rows, head_dim), bf16),
             pltpu.VMEM((total_rows, head_dim), bf16),

time: 17.2 us -> 16.4 us (0.953)
  Pallas kernels: 16.4 us -> 15.6 us
    pallas_call x1, Pallas kernels: 16.4 us -> 15.6 us  [on_device(): pl.pallas_call(functools.partial(kernel, dims), out_shape=pltpu.VMEM(quer...]
where the time goes in v3:
time: 16.4 us; the launch traced here: 16.2 us
  Pallas kernels  15.6 us (95%)
  local copies, waits for them, and re-layouts  0.6 us (4%)
    pallas_call x1, Pallas kernels, on_device(): pl.pallas_call(functools.partial(kernel, dims), out_shape=pltpu.VMEM(quer...  15.6 us
    unnamed x1, local copies, waits for them, and re-layouts  0.6 us

profile of v3, /device:TPU:0, one launch (start us, length us, event | category | flops | bytes accessed | tf_op | source)
XLA Modules:
  0.0 16.2 jit_solution(11642895770802988554)
XLA Ops:
  0.0 15.6 %shard_map.82 = bf16[1,32,128]{2,1,0:T(8,128)(2,1)S(1)} custom-call(bf16[1,32,128]{2,1,0:T(8,128)(2,1)} %q_ref.1, bf16[1024,128]{1,0:T(8,128)(2,1)} %bitcast.3, bf16[1024,128]{1,0:T(8,128)(2,1)} %bitcast.4, bf16[384,128]{1,0:T(8,128)(2,1)} %bitcast.5, s32[3,8]{1,0:T(4,128)} %owner_hbm.1, s32[3,8]{1,0:T(4,128)} %slot_hbm.1, s32[3]{0:T(128)} %len_hbm.1, ...), custom_call_target="tpu_custom_call" | custom-call | tf_op jit(solution)/shard_map/pallas_call | solution.py:313
  15.6 0.6 %copy.10 = bf16[1,32,128]{2,1,0:T(8,128)(2,1)} copy(bf16[1,32,128]{2,1,0:T(8,128)(2,1)S(1)} %shard_map.82) | data formatting | bytes 16384

commit v4 on v3

--- a/solution.py
+++ b/solution.py
@@ -77,7 +77,7 @@
         return n - 1 - side * half - lax.rem(local + k, half)
 
     def near_peer(k):
-        return side * half + lax.rem(local + k + 1, half)
+        return side * half + lax.rem(local + half - 1 - k, half)
 
     def far_peers(body):
         repeat(half, lambda k: body(k, far_peer(k)))
@@ -260,11 +260,11 @@
     near_peers(lambda k, peer: query_copy(k, peer, peer).wait_recv())
     attend(side)
     near_peers(send)
-    o_recv[me] = o_send[own_rows]
-    s_recv[me] = s_send[own_rows]
     far_peers(lambda k, peer: query_copy(k, peer, peer).wait_recv())
     attend(1 - side)
     far_peers(send)
+    o_recv[me] = o_send[own_rows]
+    s_recv[me] = s_send[own_rows]
 
     def receive(k, peer):
         s_copy(k, peer, me, peer).wait_recv()

time: 16.4 us -> 16.4 us (level)
  no operation moved by 1% of the time
where the time goes in v4:
time: 16.4 us; the launch traced here: 16.2 us
  Pallas kernels  15.6 us (95%)
  local copies, waits for them, and re-layouts  0.6 us (4%)
    pallas_call x1, Pallas kernels, on_device(): pl.pallas_call(functools.partial(kernel, dims), out_shape=pltpu.VMEM(quer...  15.6 us
    unnamed x1, local copies, waits for them, and re-layouts  0.6 us

profile of v4, /device:TPU:0, one launch (start us, length us, event | category | flops | bytes accessed | tf_op | source)
XLA Modules:
  0.0 16.2 jit_solution(2695046560210606290)
XLA Ops:
  0.0 15.6 %shard_map.82 = bf16[1,32,128]{2,1,0:T(8,128)(2,1)S(1)} custom-call(bf16[1,32,128]{2,1,0:T(8,128)(2,1)} %q_ref.1, bf16[1024,128]{1,0:T(8,128)(2,1)} %bitcast.3, bf16[1024,128]{1,0:T(8,128)(2,1)} %bitcast.4, bf16[384,128]{1,0:T(8,128)(2,1)} %bitcast.5, s32[3,8]{1,0:T(4,128)} %owner_hbm.1, s32[3,8]{1,0:T(4,128)} %slot_hbm.1, s32[3]{0:T(128)} %len_hbm.1, ...), custom_call_target="tpu_custom_call" | custom-call | tf_op jit(solution)/shard_map/pallas_call | solution.py:313
  15.6 0.6 %copy.10 = bf16[1,32,128]{2,1,0:T(8,128)(2,1)} copy(bf16[1,32,128]{2,1,0:T(8,128)(2,1)S(1)} %shard_map.82) | data formatting | bytes 16384
